TPU v7x, 32 devices: a whole 2x2x4 slice. The times are simulated.
32 devices in a mesh: grp: 4 (over y, x), dev: 8 (over z, core).
Axes of the slice: x: 2, y: 2, z: 4, core: 2. Of those that a mesh axis runs over, the one named last changes fastest.
Arguments:
- pool_latent: bfloat16 [512, 256, 512], P(('grp', 'dev')), may hold values from -6 to 6
- pool_rope: bfloat16 [512, 64, 256], P(('grp', 'dev')), may hold values from -6 to 6
- q_nope: bfloat16 [1024, 16384], P(None, 'dev'), may hold values from -6 to 6
- q_rope: bfloat16 [1024, 8192], P(None, 'dev'), may hold values from -9 to 9
- w_uk: bfloat16 [512, 16384], P(None, 'dev'), may hold values from -0.25 to 0.25
- w_uv: bfloat16 [512, 16384], P(None, 'dev'), may hold values from -0.25 to 0.25
- w_o: bfloat16 [16384, 7168], P('dev'), may hold values from -0.046875 to 0.046875
- block_table: int32 [64, 8], replicated, may hold values from 0 to 511, as said below
- lengths: int32 [64], replicated, may hold values from 2 to 2048, as said below
- preempted: int32 [32], replicated, may hold values from 0 to 63, as said below
- assignment: int32 [32], replicated, may hold values from 0 to 3, as said below
Outputs:
- mixed: bfloat16 [1024, 7168], P('grp', 'dev')
Inputs may be any that keep to these rules, and one draw needn't show every extreme that they name: `preempted`: distinct slots. `assignment`: each group receives exactly 8 requests. `block_table`: every page number 0 to 511 appears exactly once in the table; page p lies on the device with index p // 16 along grp+dev, at position p % 16 there. For every group and every index along dev, exactly 8 of the pages listed for the slots of that group's requests lie on devices with that index along dev. `lengths`: in every draw all requests of one group hold more than (7) * 256 tokens.
All inputs are finite; a program needn't handle non-finite values.
Results may differ from a plain program's by a relative error of at most 0.015.
Values may be sent and summed in bfloat16 or wider, within the bound.
A program may use at most 256 MiB of HBM per device.

v0:
```python
import math

import jax
import jax.numpy as jnp
from jax import lax
from jax.sharding import PartitionSpec as P

DR = 64
DN = 128
DV = 128


NEG = -1e30


def place_values(targets, values, length, dtype):
    return jnp.zeros((length + 1,), dtype).at[targets].set(values)[:length]


def local(
    pool_latent,
    pool_rope,
    q_nope,
    q_rope,
    w_uk,
    w_uv,
    w_o,
    block_table,
    lengths,
    preempted,
    assignment,
):
    groups = lax.axis_size("grp")
    columns = lax.axis_size("dev")
    group = lax.axis_index("grp")
    column = lax.axis_index("dev")
    pages_dev = pool_latent.shape[0]
    block = pool_latent.shape[1]
    latent_width = pool_latent.shape[2]
    rope_width = pool_rope.shape[1]
    requests = preempted.shape[0]
    blocks = block_table.shape[1]
    per_group = requests // groups
    group_pages = per_group * blocks
    per_column = group_pages // columns
    query_rows = q_nope.shape[0] // requests
    heads_dev = q_rope.shape[1] // rope_width
    scale = 1.0 / math.sqrt(DN + DR)
    slot_pages = block_table[preempted]
    slot_len = lengths[preempted]
    req_ids = jnp.arange(requests, dtype=jnp.int32)
    earlier = (assignment[:, None] == assignment[None, :]) & (req_ids[None, :] < req_ids[:, None])
    rank = jnp.sum(earlier.astype(jnp.int32), axis=1)
    entries = requests * blocks
    entry_ids = jnp.arange(entries, dtype=jnp.int32)
    entry_page = slot_pages.reshape(entries)
    entry_req = entry_ids // blocks
    entry_block = entry_ids % blocks
    entry_group = assignment[entry_req]
    holder = entry_page // pages_dev
    entry_row = holder // columns
    entry_col = holder % columns
    entry_local = entry_page % pages_dev
    entry_key = entry_col * groups + entry_group
    before = (entry_key[:, None] == entry_key[None, :]) & (entry_ids[None, :] < entry_ids[:, None])
    entry_slot = jnp.sum(before.astype(jnp.int32), axis=1)
    entry_pos = entry_col * per_column + entry_slot
    entry_valid = jnp.clip(slot_len[entry_req] - entry_block * block, 0, block)
    outgoing = groups * per_column
    sending = (entry_row == group) & (entry_col == column)
    send_target = jnp.where(sending, entry_group * per_column + entry_slot, outgoing)
    send_index = place_values(send_target, entry_local, outgoing, jnp.int32)
    send_live = place_values(send_target, jnp.ones((entries,), jnp.bool_), outgoing, jnp.bool_)
    zero = jnp.zeros((), pool_latent.dtype)
    out_latent = jnp.where(send_live[:, None, None], pool_latent[send_index], zero)
    out_rope = jnp.where(send_live[:, None, None], pool_rope[send_index], zero)
    got_latent, got_rope = (
        lax.all_to_all(out_latent, "grp", split_axis=0, concat_axis=0, tiled=True),
        lax.all_to_all(out_rope, "grp", split_axis=0, concat_axis=0, tiled=True),
    )
    mine = (entry_group == group) & (entry_col == column)
    source = place_values(jnp.where(mine, entry_slot, per_column), entry_row, per_column, jnp.int32)
    pick = source * per_column + jnp.arange(per_column, dtype=jnp.int32)
    own_latent = got_latent[pick]
    own_rope = got_rope[pick]
    in_group = entry_group == group
    pos_target = jnp.where(in_group, entry_pos, group_pages)
    page_req = place_values(pos_target, rank[entry_req], group_pages, jnp.int32)
    page_valid = place_values(pos_target, entry_valid, group_pages, jnp.int32)
    members = place_values(
        jnp.where(assignment == group, rank, per_group), req_ids, per_group, jnp.int32
    )
    rows = (
        members[:, None] * query_rows + jnp.arange(query_rows, dtype=jnp.int32)[None, :]
    ).reshape(-1)
    query_lo = q_nope[rows].reshape(per_group * query_rows, heads_dev, DN)
    query_hi = q_rope[rows].reshape(per_group, query_rows, heads_dev, rope_width)
    w_key = w_uk.reshape(latent_width, heads_dev, DN)
    q_lat = jnp.einsum("qhn,chn->qhc", query_lo, w_key, preferred_element_type=jnp.float32).astype(
        jnp.bfloat16
    )
    q_lat = q_lat.reshape(per_group, query_rows, heads_dev, latent_width)
    request_ids = jnp.arange(per_group, dtype=jnp.int32)
    token_ids = jnp.arange(block, dtype=jnp.int32)
    start_top = jnp.full((per_group, query_rows, heads_dev), NEG, jnp.float32)
    latent_piece = lax.all_gather(own_latent, "dev", axis=0, tiled=True)
    rope_piece = lax.all_gather(own_rope, "dev", axis=0, tiled=True)
    score = jnp.einsum(
        "pqhc,pkc->pqhk", q_lat[page_req], latent_piece, preferred_element_type=jnp.float32
    )
    score = score + jnp.einsum(
        "pqhr,prk->pqhk", query_hi[page_req], rope_piece, preferred_element_type=jnp.float32
    )
    score = score * scale
    live = token_ids[None, None, None, :] < page_valid[:, None, None, None]
    score = jnp.where(live, score, NEG)
    onehot = page_req[:, None] == request_ids[None, :]
    page_top = jnp.max(score, axis=3)
    piece_top = jnp.max(jnp.where(onehot[:, :, None, None], page_top[:, None], NEG), axis=0)
    top_new = jnp.maximum(start_top, piece_top)
    expo = jnp.where(live, jnp.exp(score - top_new[page_req][..., None]), 0.0)
    select = onehot.astype(jnp.float32)
    total_new = jnp.einsum(
        "pr,pqh->rqh", select, jnp.sum(expo, axis=3), precision=lax.Precision.HIGHEST
    )
    values = jnp.einsum(
        "pqhk,pkc->pqhc",
        expo.astype(jnp.bfloat16),
        latent_piece,
        preferred_element_type=jnp.float32,
    )
    acc_new = jnp.einsum("pr,pqhc->rqhc", select, values, precision=lax.Precision.HIGHEST)
    o_lat = (
        (acc_new / total_new[..., None])
        .astype(jnp.bfloat16)
        .reshape(per_group * query_rows, heads_dev, latent_width)
    )
    w_val = w_uv.reshape(latent_width, heads_dev, DV)
    heads_out = jnp.einsum("qhc,chv->qhv", o_lat, w_val, preferred_element_type=jnp.float32).astype(
        jnp.bfloat16
    )
    heads_out = heads_out.reshape(per_group * query_rows, heads_dev * DV)
    mixed = lax.psum_scatter(
        lax.dot_general(
            w_o, heads_out, (((0,), (1,)), ((), ())), preferred_element_type=jnp.float32
        ),
        "dev",
        scatter_dimension=0,
        tiled=True,
    )
    return mixed.T.astype(jnp.bfloat16)


def solution(mesh):
    in_specs = (
        P(("grp", "dev"), None, None),
        P(("grp", "dev"), None, None),
        P(None, "dev"),
        P(None, "dev"),
        P(None, "dev"),
        P(None, "dev"),
        P("dev", None),
        P(),
        P(),
        P(),
        P(),
    )
    out_specs = P("grp", "dev")
    return jax.shard_map(local, mesh=mesh, in_specs=in_specs, out_specs=out_specs, check_vma=False)
```

profile of v0, /device:TPU:0, one launch (start us, length us, event | category | flops | bytes accessed | tf_op | source)
XLA Modules:
  0.0 611.5 jit_solution(11005517029567202148)
XLA Ops:
  6.5 1.8 fusion.57
  8.4 2.1 fusion.56
  11.3 0.7 compare_select_fusion.9
  12.0 0.8 copy.48
  12.8 0.6 gather_fusion
  13.3 0.1 reshape.456
  13.4 0.1 reshape.455
  13.5 4.3 select_select_fusion.2
  17.9 15.7 %broadcast_multiply_fusion = (s32[256]{0:T(256)S(1)}, s32[256]{0:T(256)S(1)}) fusion(pred[256]{0:T(512)(128)(4,1)S(1)} %compare_reduce_fusion, pred[256]{0:T(512)(128)(4,1)S(1)} %compare_reduce_fusion.1, pred[256]{0:T(512)(128)(4,1)S(1)} %compare_reduce_fusion.2, pred[256]{0:T(512)(128)(4,1)S(1)} %compare_reduce_fusion.3, ...), kind=kLoop, calls=%fused_computation.146 | loop fusion | flops 6656 | bytes 9572 | tf_op jit(solution)/shard_map/mul | solution.py:71
  33.7 0.2 convert_reduce_fusion
  33.9 1.4 scatter_custom_fusion.4
  35.3 7.0 %gather_fusion.4 = bf16[32,256,512]{2,1,0:T(8,128)(2,1)} fusion(bf16[16,256,512]{2,1,0:T(8,128)(2,1)} %param.11, s32[1024]{0:T(1024)S(1)} %pad_clamp_fusion.1), kind=kCustom, calls=%fused_computation.4 | custom fusion | bytes 16777344 | tf_op jit(solution)/shard_map/gather | solution.py:75
  42.4 1.5 scatter_custom_fusion.3
  43.9 7.2 %broadcast_select_fusion = bf16[32,256,512]{2,1,0:T(8,128)(2,1)} fusion(bf16[32,256,512]{2,1,0:T(8,128)(2,1)} %gather_fusion.4, pred[32]{0:T(512)(128)(4,1)S(1)} %bitcast.172), kind=kLoop, calls=%fused_computation.32 | loop fusion | flops 4194304 | bytes 16777248 | tf_op jit(solution)/shard_map/jit(_where)/select_n | solution.py:75
  51.1 5.7 all-to-all-start
  56.8 1.4 scatter_custom_fusion.5
  58.2 92.3 %all-to-all-done = bf16[32,256,512]{2,1,0:T(8,128)(2,1)} async-done(((bf16[32,256,512]{2,1,0:T(8,128)(2,1)}), bf16[32,256,512]{2,1,0:T(8,128)(2,1)}, u32[]{:S(2)}, u32[]{:S(2)}) %all-to-all-start) | async-done | bytes 8388640 | tf_op jit(solution)/shard_map/all_to_all | solution.py:78
  150.6 5.4 gather_fusion.5
  156.0 1.7 gather_fusion.8
  157.7 1.1 broadcast_select_fusion.1
  158.8 4.2 all-to-all-start.1
  163.0 0.0 all-gather.7.cloned.1.call-start
  163.1 0.2 convert_reduce_fusion.1
  163.3 0.9 scatter_custom_fusion.2
  164.2 0.1 iota_add_fusion
  164.2 0.1 add.238
  164.3 5.8 gather_fusion.2
  170.1 1.3 convolution_convert_fusion
  171.4 4.7 copy.51
  176.1 1.2 gather_fusion.6
  177.3 0.7 reshape.460
  177.9 0.7 fusion.55
  178.6 4.6 select_select_fusion.1
  183.2 0.7 fusion.54
  183.9 15.8 %select_select_fusion.3 = s32[256]{0:T(256)S(1)} fusion(pred[256]{0:T(512)(128)(4,1)S(1)} %compare_reduce_fusion, pred[256]{0:T(512)(128)(4,1)S(1)} %compare_reduce_fusion.1, pred[256]{0:T(512)(128)(4,1)S(1)} %compare_reduce_fusion.2, pred[256]{0:T(512)(128)(4,1)S(1)} %compare_reduce_fusion.3, pred[256]{0:T(512)(128)(4,1)S(1)} %compare_reduce_fusion.4, ...), kind=kLoop, calls=%fused_computation.137 | loop fusion | flops 6400 | bytes 8548 | tf_op jit(solution)/shard_map/gather | solution.py:88
  199.8 1.4 scatter_custom_fusion
  201.2 14.2 %gather_fusion.3 = bf16[64,32,16,512]{3,2,1,0:T(8,128)(2,1)} fusion(bf16[8,32,16,512]{3,2,1,0:T(8,128)(2,1)} %copy.51, s32[1024]{0:T(1024)S(1)} %pad_clamp_fusion.2), kind=kCustom, calls=%fused_computation.3 | custom fusion | bytes 67109120 | tf_op jit(solution)/shard_map/gather | solution.py:109
  215.4 5.2 gather_fusion.7
  220.6 0.7 gather_fusion.1
  221.3 0.7 fusion.53
  222.0 0.7 fusion.52
  222.8 4.2 select_select_fusion
  227.0 15.6 %fusion.39 = s32[256]{0:T(256)S(1)} fusion(pred[256]{0:T(512)(128)(4,1)S(1)} %compare_reduce_fusion, pred[256]{0:T(512)(128)(4,1)S(1)} %compare_reduce_fusion.1, pred[256]{0:T(512)(128)(4,1)S(1)} %compare_reduce_fusion.2, pred[256]{0:T(512)(128)(4,1)S(1)} %compare_reduce_fusion.3, pred[256]{0:T(512)(128)(4,1)S(1)} %compare_reduce_fusion.4, ...), kind=kLoop, calls=%fused_computation.141 | loop fusion | flops 8704 | bytes 8548 | tf_op jit(solution)/shard_map/jit(clip)/min | solution.py:68
  242.6 1.4 scatter_custom_fusion.1
  244.0 3.9 copy.65
  248.0 0.1 iota_compare_fusion.1
  248.1 2.5 gather_fusion.9
  250.6 0.4 reduce-scatter.2.cloned.1.call-start
  251.0 56.7 %all-gather.5.cloned.1.call-done = bf16[64,256,512]{2,1,0:T(8,128)(2,1)} async-done(((bf16[8,256,512]{2,1,0:T(8,128)(2,1)}), bf16[64,256,512]{2,1,0:T(8,128)(2,1)}) %all-gather.5.cloned.1.call-update) | async-done | bytes 16777232 | tf_op jit(solution)/shard_map/all_gather | solution.py:106
  307.8 28.2 %fusion.7 = f32[64,32,16,256]{3,2,1,0:T(8,128)} fusion(bf16[64,32,16,512]{3,2,1,0:T(8,128)(2,1)} %gather_fusion.3, bf16[64,256,512]{2,1,0:T(8,128)(2,1)} %all-gather.5.cloned.1.call-done), kind=kOutput, calls=%fused_computation.25 | convolution fusion | flops 8589934592 | bytes 83886080 | tf_op jit(solution)/shard_map/pqhc,pkc->pqhk/dot_general | solution.py:108
  336.0 0.8 all-gather.7.cloned.1.call-done
  336.7 30.7 %fusion.58 = (f32[64,32,16]{2,1,0:T(8,128)S(1)}, f32[64,32,16,256]{3,2,1,0:T(8,128)}) fusion(f32[64,32,16,256]{3,2,1,0:T(8,128)} %fusion.7, bf16[64,32,16,64]{3,2,1,0:T(8,128)(2,1)} %gather_fusion.7, bf16[64,64,256]{2,1,0:T(8,128)(2,1)} %all-gather.7.cloned.1.call-done, pred[64,256]{1,0:T(8,128)(4,1)S(1)} %iota_compare_fusion.1), kind=kOutput, calls=%fused_computation.173 | convolution fusion | flops 1107263488 | bytes 73547776 | tf_op jit(solution)/shard_map/pqhr,prk->pqhk/dot_general | solution.py:111
  367.4 0.6 copy.52
  368.0 0.6 select_reduce_fusion
  368.7 0.6 gather_fusion.10
  369.3 16.4 %fusion.2 = f32[64,32,16]{2,1,0:T(8,128)S(1)} fusion(f32[64,32,16,256]{3,2,1,0:T(8,128)} %get-tuple-element.114, f32[64,32,16]{2,1,0:T(8,128)S(1)} %gather_fusion.10, pred[64,256]{1,0:T(8,128)(4,1)S(1)} %iota_compare_fusion.1), kind=kLoop, calls=%fused_computation.21 | loop fusion | flops 25133056 | bytes 33832960 | tf_op jit(solution)/shard_map/reduce_sum | solution.py:124
  385.7 1.3 fusion.24
  387.0 39.9 %fusion.4 = f32[64,32,16,512]{3,2,1,0:T(8,128)} fusion(f32[64,32,16,256]{3,2,1,0:T(8,128)} %get-tuple-element.114, bf16[64,256,512]{2,1,0:T(8,128)(2,1)} %all-gather.5.cloned.1.call-done, f32[64,32,16]{2,1,0:T(8,128)S(1)} %gather_fusion.10, pred[64,256]{1,0:T(8,128)(4,1)S(1)} %iota_compare_fusion.1), kind=kOutput, calls=%fused_computation.23 | convolution fusion | flops 8615100416 | bytes 117587968 | tf_op jit(solution)/shard_map/pqhk,pkc->pqhc/dot_general | solution.py:126
  426.9 73.7 %divide_convert_fusion = bf16[8,32,16,512]{3,0,2,1:T(8,128)(2,1)} fusion(f32[8,32,16]{0,2,1:T(8,128)S(1)} %fusion.24, f32[64,32,16,512]{3,2,1,0:T(8,128)} %fusion.4, s32[64]{0:T(128)S(1)} %get-tuple-element.15), kind=kOutput, calls=%fused_computation.31 | convolution fusion | flops 1614807552 | bytes 71319808 | tf_op jit(solution)/shard_map/pr,pqhc->rqhc/dot_general | solution.py:132
  500.7 3.7 copy.56
  504.5 2.5 fusion.19
  507.0 16.6 %convolution_bitcast_fusion = f32[7168,256]{0,1:T(8,128)} fusion(bf16[256,2048]{0,1:T(8,128)(2,1)S(1)} %bitcast.164, bf16[2048,7168]{1,0:T(8,128)(2,1)} %param.17), kind=kOutput, calls=%fused_computation.30 | convolution fusion | flops 7516192768 | bytes 37748736 | tf_op jit(solution)/shard_map/dot_general | solution.py:144
  523.6 79.2 %reduce-scatter.2.cloned.1.call-done = f32[896,256]{0,1:T(8,128)} async-done(((f32[7168,256]{0,1:T(8,128)}), f32[896,256]{0,1:T(8,128)}) %reduce-scatter.2.cloned.1.call-update) | async-done | bytes 917520 | tf_op jit(solution)/shard_map/reduce_scatter | solution.py:143
  602.8 2.0 convert_bitcast_fusion
  (62 shorter events, 1.2 us)
Async XLA Ops:
  6.5 163.6 %copy-start = (bf16[512,2048]{1,0:T(8,128)(2,1)S(1)}, bf16[512,2048]{1,0:T(8,128)(2,1)}, u32[]{:S(2)}) copy-start(bf16[512,2048]{1,0:T(8,128)(2,1)} %param.15) | copy-start | bytes 6291460
  51.1 99.5 %all-to-all-start = ((bf16[32,256,512]{2,1,0:T(8,128)(2,1)}), bf16[32,256,512]{2,1,0:T(8,128)(2,1)}, u32[]{:S(2)}, u32[]{:S(2)}) async-start(bf16[32,256,512]{2,1,0:T(8,128)(2,1)} %broadcast_select_fusion), calls=%async_computation | async-start | bytes 16777216 | tf_op jit(solution)/shard_map/all_to_all | solution.py:78
  56.7 106.3 %copy-start.5 = (s32[32]{0:T(128)S(1)}, s32[32]{0:T(128)}, u32[]{:S(2)}) copy-start(s32[32]{0:T(128)} %param.21) | copy-start | bytes 388
  56.8 251.0 %all-gather.5.cloned.1.call-start = ((), (), s32[]{:S(2)}) async-start(), calls=%async_computation.4 | async-start | bytes 18874368 | tf_op jit(solution)/shard_map/all_gather | solution.py:106
  158.8 89.3 %all-to-all-start.1 = ((bf16[32,64,256]{2,1,0:T(8,128)(2,1)}), bf16[32,64,256]{2,1,0:T(8,128)(2,1)}, u32[]{:S(2)}, u32[]{:S(2)}) async-start(bf16[32,64,256]{2,1,0:T(8,128)(2,1)} %broadcast_select_fusion.1), calls=%async_computation.1 | async-start | bytes 2097152 | tf_op jit(solution)/shard_map/all_to_all | solution.py:79
  163.0 173.7 %all-gather.7.cloned.1.call-start = ((), (), s32[]{:S(2)}) async-start(), calls=%async_computation.5 | async-start | bytes 2359296 | tf_op jit(solution)/shard_map/all_gather | solution.py:107
  171.4 4.7 copy-start.3
  215.4 5.2 copy-start.2
  250.6 352.2 %reduce-scatter.2.cloned.1.call-start = ((), (), s32[]{:S(2)}) async-start(), calls=%async_computation.3 | async-start | bytes 8257536 | tf_op jit(solution)/shard_map/reduce_scatter | solution.py:143
  500.7 3.8 copy-start.4
  507.0 97.8 %copy-start.1 = (bf16[512,2048]{1,0:T(8,128)(2,1)S(1)}, bf16[512,2048]{1,0:T(8,128)(2,1)}, u32[]{:S(2)}) copy-start(bf16[512,2048]{1,0:T(8,128)(2,1)} %param.15) | copy-start | bytes 6291460
Sparse Core Ops, SparseCore 0:
  156.1 151.5 all-gather.4
  309.4 27.3 all-gather.6
  523.7 78.9 reduce-scatter.1
where the time goes:
time: 618 us; the launch traced here: 612 us
  waiting for transfers between devices  229 us (37%)
  matrix products  194 us (31%)
  other arithmetic  89.9 us (15%)
  local copies, waits for them, and re-layouts  74.2 us (12%)
  between operations  13.7 us (2%)
  starting transfers between devices  10.4 us (2%)
    all_to_all x1, waiting for transfers between devices, local(): lax.all_to_all(out_latent, 'grp', split_axis=0, concat_axis=0, tiled=True)  92.3 us
    reduce_scatter x1, waiting for transfers between devices, local(): lax.psum_scatter(lax.dot_general(w_o, heads_out, (((0,), (1,)), ((), ()))...  79.2 us
    dot_general x1, matrix products, local(): jnp.einsum('pr,pqhc->rqhc', select, values, precision=lax.Precision.HIGHEST)  73.7 us
    all_gather x1, waiting for transfers between devices, local(): latent_piece = lax.all_gather(own_latent, 'dev', axis=0, tiled=True)  56.7 us
    dot_general x1, matrix products, local(): jnp.einsum('pqhk,pkc->pqhc', expo.astype(jnp.bfloat16), latent_piece, pre...  39.9 us
    dot_general x1, matrix products, local(): jnp.einsum('pqhr,prk->pqhk', query_hi[page_req], rope_piece, preferred_el...  30.7 us
    dot_general x1, matrix products, local(): jnp.einsum('pqhc,pkc->pqhk', q_lat[page_req], latent_piece, preferred_ele...  28.2 us
    gather x2, other arithmetic, local(): page_req = place_values(pos_target, rank[entry_req], group_pages, jnp.int32)  20.4 us
  transfers between devices with their start and end apart: 5, of which 4 were waited for; matrix products, arithmetic and copies ran while one was open for 20% of the time, Pallas kernels for 0%

commit v1 on v0

v1 whole, which is shorter than its diff:
```python
import functools
import math

import jax
import jax.numpy as jnp
from jax import lax
from jax.experimental import pallas as pl
from jax.experimental.pallas import tpu as pltpu
from jax.sharding import PartitionSpec as P

DR = 64
DN = 128
DV = 128
CHUNKS = 2
ROWS = 256

NEG = -1e30


def choose(onehot, values):
    return jnp.sum(jnp.where(onehot, values, 0), axis=-1, dtype=jnp.int32)


def attend(first, last, offset, blocks, block, span, scale, where, sizes, *refs):
    q_ref, qr_ref = refs[:2]
    pages = refs[2 : 2 + blocks]
    refs = refs[2 + blocks :]
    if not first:
        acc_in, top_in, sum_in = refs[:3]
        refs = refs[3:]
    if last:
        out_ref = refs[0]
        refs = refs[1:]
    else:
        acc_out, top_out, sum_out = refs[:3]
        refs = refs[3:]
    lat, rope = refs
    width = lat.shape[1]
    heads, count, _ = q_ref.shape
    rope_width = rope.shape[0]
    fold = width // span
    depth = rope_width // fold
    for b in range(blocks):
        lat[b * span : (b + 1) * span, :] = pages[b][0, :span, :]
        for j in range(fold):
            rope[j * depth : (j + 1) * depth, b * span : (b + 1) * span] = pages[b][
                0, span:, j * span : (j + 1) * span
            ]
    length = sizes[pl.program_id(0)]
    token = lax.broadcasted_iota(jnp.int32, (1, blocks * span), 1)
    position = (token // span) * block + token % span + offset
    bias = jnp.where(position < length, 0.0, NEG)
    some = max(1, min(heads, ROWS // count))
    for h in range(0, heads, some):
        rows = some * count
        q = q_ref[h : h + some].reshape(rows, width)
        qr = qr_ref[h : h + some].reshape(rows, rope_width)
        score = lax.dot_general(
            q, lat[...], (((1,), (1,)), ((), ())), preferred_element_type=jnp.float32
        ) + jnp.dot(qr, rope[...], preferred_element_type=jnp.float32)
        score = score * scale + bias
        top = jnp.max(score, axis=1, keepdims=True)
        if not first:
            old = top_in[h : h + some].reshape(rows, 128)[:, :1]
            top = jnp.maximum(top, old)
        expo = jnp.exp(score - top)
        total = jnp.sum(expo, axis=1, keepdims=True)
        acc = jnp.dot(expo.astype(jnp.bfloat16), lat[...], preferred_element_type=jnp.float32)
        if not first:
            fade = jnp.exp(old - top)
            total = total + fade * sum_in[h : h + some].reshape(rows, 128)[:, :1]
            acc = acc + fade * acc_in[h : h + some].reshape(rows, width)
        if last:
            out_ref[h : h + some] = (acc / total).astype(out_ref.dtype).reshape(some, count, width)
        else:
            acc_out[h : h + some] = acc.reshape(some, count, width)
            top_out[h : h + some] = jnp.broadcast_to(top, (rows, 128)).reshape(some, count, 128)
            sum_out[h : h + some] = jnp.broadcast_to(total, (rows, 128)).reshape(some, count, 128)


def attention(state, q_lat, q_hi, pages, where, sizes, block, chunk, span, scale, count, blocks):
    heads, rows, width = q_lat.shape
    rope_width = q_hi.shape[2]
    requests = rows // count
    first, last = chunk == 0, chunk == CHUNKS - 1

    def rowspec(w):
        return pl.BlockSpec((heads, count, w), lambda r, *_: (0, r, 0))

    def pagespec(b):
        return pl.BlockSpec(
            (1,) + pages.shape[1:], lambda r, where, sizes: (where[r * blocks + b], 0, 0)
        )

    in_specs = [rowspec(width), rowspec(rope_width)] + [pagespec(b) for b in range(blocks)]
    if not first:
        in_specs += [rowspec(width), rowspec(128), rowspec(128)]
    if last:
        out_specs = rowspec(width)
        out_shape = jax.ShapeDtypeStruct((heads, rows, width), jnp.bfloat16)
    else:
        out_specs = [rowspec(width), rowspec(128), rowspec(128)]
        out_shape = [
            jax.ShapeDtypeStruct((heads, rows, w), jnp.float32) for w in (width, 128, 128)
        ]
    tokens = blocks * span
    return pl.pallas_call(
        functools.partial(attend, first, last, chunk * span, blocks, block, span, scale),
        grid_spec=pltpu.PrefetchScalarGridSpec(
            num_scalar_prefetch=2,
            grid=(requests,),
            in_specs=in_specs,
            out_specs=out_specs,
            scratch_shapes=[
                pltpu.VMEM((tokens, width), jnp.bfloat16),
                pltpu.VMEM((rope_width, tokens), jnp.bfloat16),
            ],
        ),
        out_shape=out_shape,
        cost_estimate=pl.CostEstimate(
            flops=2 * heads * rows * tokens * (2 * width + rope_width),
            bytes_accessed=pages.size * 2 + heads * rows * width * 8,
            transcendentals=heads * rows * tokens,
        ),
        compiler_params=pltpu.CompilerParams(vmem_limit_bytes=48 * 1024 * 1024),
        name=f"attend{chunk}",
    )(where, sizes, q_lat, q_hi, *([pages] * blocks), *state)


def local(
    pool_latent,
    pool_rope,
    q_nope,
    q_rope,
    w_uk,
    w_uv,
    w_o,
    block_table,
    lengths,
    preempted,
    assignment,
):
    groups = lax.axis_size("grp")
    columns = lax.axis_size("dev")
    group = lax.axis_index("grp")
    column = lax.axis_index("dev")
    pages_dev, block, latent_width = pool_latent.shape
    rope_width = pool_rope.shape[1]
    requests = preempted.shape[0]
    slots, blocks = block_table.shape
    per_group = requests // groups
    group_pages = per_group * blocks
    per_column = group_pages // columns
    query_rows = q_nope.shape[0] // requests
    heads_dev = q_rope.shape[1] // rope_width
    scale = 1.0 / math.sqrt(DN + DR)
    span = block // CHUNKS
    fold = latent_width // span
    entries = requests * blocks

    hot = preempted[:, None] == jnp.arange(slots, dtype=jnp.int32)[None, :]
    slot_pages = choose(hot[:, None, :], block_table.T[None, :, :])
    slot_len = choose(hot, lengths[None, :])
    req_ids = jnp.arange(requests, dtype=jnp.int32)
    earlier = (assignment[:, None] == assignment[None, :]) & (req_ids[None, :] < req_ids[:, None])
    rank = jnp.sum(earlier.astype(jnp.int32), axis=1)
    block_ids = jnp.arange(blocks, dtype=jnp.int32)
    page = slot_pages.reshape(entries)
    used = (block_ids[None, :] * block < slot_len[:, None]).reshape(entries)
    entry_group = jnp.broadcast_to(assignment[:, None], (requests, blocks)).reshape(entries)
    entry_place = jnp.broadcast_to(rank[:, None] * blocks, (requests, blocks)).reshape(
        entries
    ) + jnp.broadcast_to(block_ids[None, :], (requests, blocks)).reshape(entries)
    ids = jnp.arange(entries, dtype=jnp.int32)
    holder = page // pages_dev
    entry_row = holder // columns
    entry_col = holder % columns
    entry_local = page % pages_dev
    ahead = ids[None, :] < ids[:, None]
    same = (entry_col * groups + entry_group)[:, None] == (entry_col * groups + entry_group)[None, :]
    entry_slot = jnp.sum((same & ahead).astype(jnp.int32), axis=1)
    same_row = same & (entry_row[:, None] == entry_row[None, :]) & used[None, :]
    entry_turn = jnp.sum((same_row & ahead).astype(jnp.int32), axis=1)
    deepest = jnp.max(jnp.where(used, entry_turn + 1, 0))

    sending = used & (entry_row == group) & (entry_col == column)
    mine = used & (entry_group == group) & (entry_col == column)
    column_ids = jnp.arange(per_column, dtype=jnp.int32)
    mine_hot = mine[None, :] & (entry_slot[None, :] == column_ids[:, None])
    from_row = choose(mine_hot, entry_row[None, :])
    from_turn = choose(mine_hot, entry_turn[None, :])
    in_group = entry_group == group
    place_ids = jnp.arange(group_pages, dtype=jnp.int32)
    where = choose(
        in_group[None, :] & (entry_place[None, :] == place_ids[:, None]),
        (entry_col * per_column + entry_slot)[None, :],
    )
    group_ids = jnp.arange(per_group, dtype=jnp.int32)
    member_hot = (assignment == group)[None, :] & (rank[None, :] == group_ids[:, None])
    members = choose(member_hot, req_ids[None, :])
    sizes = choose(member_hot, slot_len[None, :])

    def exchange(chunk, capacity, _):
        turns = jnp.arange(groups * capacity, dtype=jnp.int32)
        target = jnp.where(
            sending & (entry_turn < capacity), entry_group * capacity + entry_turn, -1
        )
        index = choose(target[None, :] == turns[:, None], entry_local[None, :])
        part = slice(chunk * span, (chunk + 1) * span)
        rope = pool_rope[:, :, part]
        packed = jnp.concatenate(
            [
                pool_latent[:, part, :],
                jnp.concatenate(jnp.split(rope, fold, axis=1), axis=2),
            ],
            axis=1,
        )
        out = packed[index]
        got = lax.all_to_all(out, "grp", split_axis=0, concat_axis=0, tiled=True)
        return got[from_row * capacity + from_turn]

    capacities = [c for c in (4, 5, 6) if c < per_column] + [per_column]
    branch = jnp.sum(jnp.array([deepest > c for c in capacities[:-1]], jnp.int32)) if len(
        capacities
    ) > 1 else None

    own = []
    for chunk in range(CHUNKS):
        forms = [functools.partial(exchange, chunk, c) for c in capacities]
        own.append(forms[0](0) if branch is None else lax.switch(branch, forms, jnp.int32(0)))
    gathered = [lax.all_gather(o, "dev", axis=0, tiled=True) for o in own]

    query_lo = q_nope.reshape(requests, query_rows, heads_dev * DN)[members]
    query_hi = q_rope.reshape(requests, query_rows, heads_dev * rope_width)[members]
    query_lo = query_lo.reshape(per_group * query_rows, heads_dev, DN)
    query_hi = query_hi.reshape(per_group * query_rows, heads_dev, rope_width).transpose(1, 0, 2)
    w_key = w_uk.reshape(latent_width, heads_dev, DN)
    q_lat = jnp.einsum("qhn,chn->hqc", query_lo, w_key, preferred_element_type=jnp.float32).astype(
        jnp.bfloat16
    )

    state = ()
    for chunk in range(CHUNKS):
        state = attention(
            state,
            q_lat,
            query_hi,
            gathered[chunk],
            where,
            sizes,
            block,
            chunk,
            span,
            scale,
            query_rows,
            blocks,
        )
    o_lat = state
    w_val = w_uv.reshape(latent_width, heads_dev, DV)
    heads_out = jnp.einsum("hqc,chv->qhv", o_lat, w_val, preferred_element_type=jnp.float32).astype(
        jnp.bfloat16
    )
    heads_out = heads_out.reshape(per_group * query_rows, heads_dev * DV)
    mixed = lax.psum_scatter(
        lax.dot_general(
            w_o, heads_out, (((0,), (1,)), ((), ())), preferred_element_type=jnp.float32
        ).astype(jnp.bfloat16),
        "dev",
        scatter_dimension=0,
        tiled=True,
    )
    return mixed.T


def solution(mesh):
    in_specs = (
        P(("grp", "dev"), None, None),
        P(("grp", "dev"), None, None),
        P(None, "dev"),
        P(None, "dev"),
        P(None, "dev"),
        P(None, "dev"),
        P("dev", None),
        P(),
        P(),
        P(),
        P(),
    )
    out_specs = P("grp", "dev")
    return jax.shard_map(local, mesh=mesh, in_specs=in_specs, out_specs=out_specs, check_vma=False)
```

time: 618 us -> 346 us (0.56); the launches traced: 612 us -> 349 us
  matrix products: 194 us -> 22.9 us
  other arithmetic: 89.9 us -> 8.22 us
  Pallas kernels: 0 us -> 42.5 us
  local copies, waits for them, and re-layouts: 74.2 us -> 46.3 us
  waiting for transfers between devices: 229 us -> 203 us
    dot_general x7 -> x2, matrix products: 178 us -> 8.3 us  [the longest x1 4.63 us: local(): jnp.einsum('qhn,chn->hqc', query_lo, w_key, preferred_element_type=jnp.fl...]
    reduce_scatter x1 -> x0, waiting for transfers between devices: 79.2 us -> none  [local(): lax.psum_scatter(lax.dot_general(w_o, heads_out, (((0,), (1,)), ((), ()))...]
    unnamed x3 -> x4, waiting for transfers between devices: 0.05 us -> 43.6 us
    pallas_call x0 -> x2, Pallas kernels: none -> 42.5 us  [attention(): pl.pallas_call(functools.partial(attend, first, last, chunk * span, block...]
    all_gather x2, waiting for transfers between devices: 57.5 us -> 90.9 us  [local(): gathered = [lax.all_gather(o, 'dev', axis=0, tiled=True) for o in own]]
    gather x17 -> x6, local copies, waits for them, and re-layouts: 51.6 us -> 18.3 us  [the longest x2 8.29 us: exchange(): out = packed[index]]
    gather x34 -> x5, other arithmetic: 29.9 us -> 0.04 us  [the longest x2 0.02 us: exchange(): out = packed[index]]
    all_to_all x2, waiting for transfers between devices: 92.3 us -> 68.8 us  [exchange(): got = lax.all_to_all(out, 'grp', split_axis=0, concat_axis=0, tiled=True)]
  transfers between devices with their start and end apart: 5 -> 5, of which waited for: 4 -> 5; matrix products, arithmetic and copies ran while one was open for 20% -> 9% of each run, Pallas kernels for 0% -> 6%
where the time goes in v1:
time: 346 us; the launch traced here: 349 us
  waiting for transfers between devices  203 us (59%)
  local copies, waits for them, and re-layouts  46.3 us (13%)
  Pallas kernels  42.5 us (12%)
  matrix products  22.9 us (7%)
  between operations  15.2 us (4%)
  starting transfers between devices  10.2 us (3%)
  other arithmetic  8.22 us (2%)
    all_gather x2, waiting for transfers between devices, local(): gathered = [lax.all_gather(o, 'dev', axis=0, tiled=True) for o in own]  90.9 us
    all_to_all x2, waiting for transfers between devices, exchange(): got = lax.all_to_all(out, 'grp', split_axis=0, concat_axis=0, tiled=True)  68.8 us
    unnamed x4, waiting for transfers between devices  43.6 us
    pallas_call x2, Pallas kernels, attention(): pl.pallas_call(functools.partial(attend, first, last, chunk * span, block...  42.5 us
    dot_general x1, matrix products, local(): lax.dot_general(w_o, heads_out, (((0,), (1,)), ((), ())), preferred_eleme...  14.6 us
    unnamed x19, local copies, waits for them, and re-layouts  14.3 us
    all_to_all x2, starting transfers between devices, exchange(): got = lax.all_to_all(out, 'grp', split_axis=0, concat_axis=0, tiled=True)  9.89 us
    gather x2, local copies, waits for them, and re-layouts, exchange(): out = packed[index]  8.29 us
  transfers between devices with their start and end apart: 5, of which 5 were waited for; matrix products, arithmetic and copies ran while one was open for 9% of the time, Pallas kernels for 6%

profile of v1, /device:TPU:0, one launch (start us, length us, event | category | flops | bytes accessed | tf_op | source)
XLA Modules:
  0.0 348.8 jit_solution(15231536978750334027)
XLA Ops:
  6.5 0.0 copy-start
  6.5 0.0 all-gather.5.cloned.1.call-start
  6.5 0.9 iota_compare_fusion.10
  7.4 0.9 select_reduce_fusion.10
  8.3 0.1 broadcast_compare_fusion
  8.3 0.1 lt.220
  8.5 0.7 broadcast_in_dim.296
  9.2 0.1 reshape.411
  9.3 1.3 select_reduce_fusion.8
  10.6 0.1 reshape.412
  10.8 0.3 convert_reduce_fusion
  11.0 0.6 select_reduce_fusion.15
  13.6 0.1 select_reduce_fusion.11
  13.8 51.3 %conditional.3 = (bf16[8,144,512]{2,1,0:T(8,128)(2,1)S(1)}) conditional(s32[]{:T(128)} %clamp.4, (bf16[16,256,512]{2,1,0:T(8,128)(2,1)}, bf16[16,64,256]{2,1,0:T(8,128)(2,1)}, s32[256]{0:T(256)S(1)}, pred[256]{0:T(512)(128)(4,1)S(1)}, s32[256]{0:T(256)S(1)}, /*index=5*/s32[256]{0:T(256)S(1)}, s32[8]{0:T(128)S(1)}, ...), branch_computations={%region_19.21_spmd, %region_21.23_spmd, %region_23.25_spmd, %regio... | conditional | flops 11824488 | bytes 35403848 | solution.py:230
  13.8 1.0 fusion.24
  14.8 1.8 slice.61
  16.6 0.1 select_reduce_fusion.5
  16.7 1.6 maximum_maximum_fusion.5
  18.3 4.2 %gather_fusion.10 = bf16[20,144,512]{2,1,0:T(8,128)(2,1)} fusion(bf16[16,144,512]{2,1,0:T(8,128)(2,1)} %maximum_maximum_fusion.5, s32[1024]{0:T(1024)S(1)} %pad_clamp_fusion.11), kind=kCustom, calls=%fused_computation.10 | custom fusion | bytes 5898320 | tf_op jit(solution)/shard_map/cond/branch_1_fun/gather | solution.py:218
  22.4 5.2 %all-to-all-start.5 = ((bf16[20,144,512]{2,1,0:T(8,128)(2,1)}), bf16[20,144,512]{2,1,0:T(8,128)(2,1)}, u32[]{:S(2)}, u32[]{:S(2)}) async-start(bf16[20,144,512]{2,1,0:T(8,128)(2,1)} %gather_fusion.10), calls=%async_computation.5 | async-start | bytes 5898240 | tf_op jit(solution)/shard_map/cond/branch_1_fun/all_to_all | solution.py:219
  27.7 35.0 %all-to-all-done.5 = bf16[20,144,512]{2,1,0:T(8,128)(2,1)} async-done(((bf16[20,144,512]{2,1,0:T(8,128)(2,1)}), bf16[20,144,512]{2,1,0:T(8,128)(2,1)}, u32[]{:S(2)}, u32[]{:S(2)}) %all-to-all-start.5) | async-done | bytes 2949152 | tf_op jit(solution)/shard_map/cond/branch_1_fun/all_to_all | solution.py:219
  62.6 2.5 gather_fusion.11
  65.1 0.0 copy-start.5
  65.1 1.0 copy-done.5
  66.1 0.0 all-gather.5.cloned.1.call-update
  66.2 0.0 copy-start.7
  66.2 0.0 all-gather.3.cloned.1.call-start
  66.2 49.8 %conditional.2 = (bf16[8,144,512]{2,1,0:T(8,128)(2,1)S(1)}) conditional(s32[]{:T(128)} %clamp.4, (bf16[16,256,512]{2,1,0:T(8,128)(2,1)}, bf16[16,64,256]{2,1,0:T(8,128)(2,1)}, s32[256]{0:T(256)S(1)}, pred[256]{0:T(512)(128)(4,1)S(1)}, s32[256]{0:T(256)S(1)}, /*index=5*/s32[256]{0:T(256)S(1)}, s32[8]{0:T(128)S(1)}, ...), branch_computations={%region_11.13_spmd, %region_13.15_spmd, %region_15.17_spmd, %regio... | conditional | flops 11824488 | bytes 35403848 | solution.py:230
  66.3 1.0 fusion.20
  67.2 1.8 slice.57
  69.1 0.1 select_reduce_fusion.1
  69.2 1.6 maximum_maximum_fusion.1
  70.8 4.1 %gather_fusion.2 = bf16[20,144,512]{2,1,0:T(8,128)(2,1)} fusion(bf16[16,144,512]{2,1,0:T(8,128)(2,1)} %maximum_maximum_fusion.1, s32[1024]{0:T(1024)S(1)} %pad_clamp_fusion.3), kind=kCustom, calls=%fused_computation.2 | custom fusion | bytes 5898320 | tf_op jit(solution)/shard_map/cond/branch_1_fun/gather | solution.py:218
  74.9 4.7 %all-to-all-start.1 = ((bf16[20,144,512]{2,1,0:T(8,128)(2,1)}), bf16[20,144,512]{2,1,0:T(8,128)(2,1)}, u32[]{:S(2)}, u32[]{:S(2)}) async-start(bf16[20,144,512]{2,1,0:T(8,128)(2,1)} %gather_fusion.2), calls=%async_computation.1 | async-start | bytes 5898240 | tf_op jit(solution)/shard_map/cond/branch_1_fun/all_to_all | solution.py:219
  79.6 33.8 %all-to-all-done.1 = bf16[20,144,512]{2,1,0:T(8,128)(2,1)} async-done(((bf16[20,144,512]{2,1,0:T(8,128)(2,1)}), bf16[20,144,512]{2,1,0:T(8,128)(2,1)}, u32[]{:S(2)}, u32[]{:S(2)}) %all-to-all-start.1) | async-done | bytes 2949152 | tf_op jit(solution)/shard_map/cond/branch_1_fun/all_to_all | solution.py:219
  113.5 2.5 gather_fusion.3
  116.1 1.0 copy-done.6
  117.1 0.0 all-gather.3.cloned.1.call-update
  117.1 0.2 reduce-scatter.4.cloned.1.call-start
  117.3 0.0 copy-done.7
  117.3 0.2 convert_reduce_fusion.2
  117.5 0.1 iota_add_fusion
  117.6 0.1 add.257
  117.7 0.1 select_reduce_fusion.13
  117.9 2.9 gather_fusion.16
  120.7 1.2 copy.30
  122.0 2.2 gather_fusion.17
  124.1 1.6 reshape.417
  125.8 1.5 copy.38
  127.3 3.9 %copy.26 = bf16[512,2048]{0,1:T(8,128)(2,1)} copy(bf16[512,2048]{1,0:T(8,128)(2,1)} %param.24) | data formatting | bytes 4194304 | tf_op jit(solution)/shard_map/reshape | solution.py:259
  131.2 0.1 select_reduce_fusion.9.where
  131.3 4.6 %convolution_convert_fusion.1.refs_0_ = bf16[16,256,512]{2,1,0:T(8,128)(2,1)} fusion(bf16[256,16,128]{2,1,0:T(8,128)(2,1)} %bitcast.68, bf16[512,2048]{1,0:T(8,128)(2,1)S(1)} %copy-done), kind=kOutput, calls=%fused_computation.92 | convolution fusion | flops 538968064 | bytes 7340032 | tf_op jit(solution)/shard_map/qhn,chn->hqc/dot_general | solution.py:238
  136.0 21.6 %all-gather.5.cloned.1.call-done.refs_2_.refs_3_.refs_4_.refs_5_.refs_6_.refs_7_.refs_8_.refs_9_ = bf16[64,144,512]{2,1,0:T(8,128)(2,1)} async-done(((bf16[8,144,512]{2,1,0:T(8,128)(2,1)}), bf16[64,144,512]{2,1,0:T(8,128)(2,1)}) %all-gather.5.cloned.1.call-update) | async-done | bytes 9437200 | tf_op jit(solution)/shard_map/all_gather | solution.py:231
  157.5 20.1 %attend0.1 = (f32[16,256,512]{2,1,0:T(8,128)}, f32[16,256,128]{2,1,0:T(8,128)S(1)}, f32[16,256,128]{2,1,0:T(8,128)S(1)}) custom-call(s32[64]{0:T(128)S(1)} %select_reduce_fusion.9.where, s32[8]{0:T(128)S(1)} %get-tuple-element.218.sizes, bf16[16,256,512]{2,1,0:T(8,128)(2,1)} %convolution_convert_fusion.1.refs_0_, bf16[16,256,64]{2,1,0:T(8,128)(2,1)S(1)} %bitcast.64, ...), custom_call_target="tpu_custom_call" | custom-call | flops 9126805504 | bytes 26214400 | tf_op jit(solution)/shard_map/attend0/pallas_call | solution.py:107
  177.6 1.3 copy-done.2
  179.0 69.4 %all-gather.3.cloned.1.call-done.refs_2_.refs_3_.refs_4_.refs_5_.refs_6_.refs_7_.refs_8_.refs_9_ = bf16[64,144,512]{2,1,0:T(8,128)(2,1)} async-done(((bf16[8,144,512]{2,1,0:T(8,128)(2,1)}), bf16[64,144,512]{2,1,0:T(8,128)(2,1)}) %all-gather.3.cloned.1.call-update) | async-done | bytes 9437200 | tf_op jit(solution)/shard_map/all_gather | solution.py:231
  248.3 1.6 copy-done.3
  249.9 22.4 %attend1.1 = bf16[16,256,512]{2,1,0:T(8,128)(2,1)} custom-call(s32[64]{0:T(128)S(1)} %select_reduce_fusion.9.where, s32[8]{0:T(128)S(1)} %get-tuple-element.218.sizes, bf16[16,256,512]{2,1,0:T(8,128)(2,1)} %convolution_convert_fusion.1.refs_0_, bf16[16,256,64]{2,1,0:T(8,128)(2,1)S(1)} %bitcast.65, ...), custom_call_target="tpu_custom_call" | custom-call | flops 9126805504 | bytes 26214400 | tf_op jit(solution)/shard_map/attend1/pallas_call | solution.py:107
  272.4 3.7 %convolution_convert_fusion.2 = bf16[16,256,128]{1,2,0:T(8,128)(2,1)S(1)} fusion(bf16[16,256,512]{2,1,0:T(8,128)(2,1)} %attend1.1, bf16[512,16,128]{0,2,1:T(8,128)(2,1)S(1)} %bitcast.66), kind=kOutput, calls=%fused_computation.95 | convolution fusion | flops 537395200 | bytes 7340032 | tf_op jit(solution)/shard_map/hqc,chv->qhv/dot_general | solution.py:260
  276.0 14.6 %fusion.8 = bf16[7168,256]{0,1:T(8,128)(2,1)} fusion(bf16[256,2048]{0,1:T(8,128)(2,1)S(1)} %bitcast.67, bf16[2048,7168]{1,0:T(8,128)(2,1)} %param.25), kind=kOutput, calls=%fused_computation.91 | convolution fusion | flops 7518027776 | bytes 34078720 | tf_op jit(solution)/shard_map/dot_general | solution.py:265
  290.7 6.0 %copy.27 = bf16[7168,256]{1,0:T(8,128)(2,1)} copy(bf16[7168,256]{0,1:T(8,128)(2,1)} %fusion.8) | data formatting | bytes 7340032
  296.7 0.0 reduce-scatter.4.cloned.1.call-update
  296.7 43.5 %reduce-scatter.4.cloned.1.call-done = bf16[896,256]{1,0:T(8,128)(2,1)} async-done(((bf16[7168,256]{1,0:T(8,128)(2,1)}), bf16[896,256]{1,0:T(8,128)(2,1)}) %reduce-scatter.4.cloned.1.call-update) | async-done | bytes 458768
  340.3 2.0 copy.28
  (28 shorter events, 0.2 us)
Async XLA Ops:
  6.5 124.8 %copy-start = (bf16[512,2048]{1,0:T(8,128)(2,1)S(1)}, bf16[512,2048]{1,0:T(8,128)(2,1)}, u32[]{:S(2)}) copy-start(bf16[512,2048]{1,0:T(8,128)(2,1)} %param.23) | copy-start | bytes 6291460
  6.5 151.0 %all-gather.5.cloned.1.call-start = ((), (), s32[]{:S(2)}) async-start(), calls=%async_computation.10 | async-start | bytes 10616832 | tf_op jit(solution)/shard_map/all_gather | solution.py:231
  22.4 40.2 %all-to-all-start.5 = ((bf16[20,144,512]{2,1,0:T(8,128)(2,1)}), bf16[20,144,512]{2,1,0:T(8,128)(2,1)}, u32[]{:S(2)}, u32[]{:S(2)}) async-start(bf16[20,144,512]{2,1,0:T(8,128)(2,1)} %gather_fusion.10), calls=%async_computation.5 | async-start | bytes 5898240 | tf_op jit(solution)/shard_map/cond/branch_1_fun/all_to_all | solution.py:219
  65.1 1.0 copy-start.5
  66.2 51.1 %copy-start.7 = (s32[32]{0:T(128)S(1)}, s32[32]{0:T(128)}, u32[]{:S(2)}) copy-start(s32[32]{0:T(128)} %param.29) | copy-start | bytes 388
  66.2 182.2 %all-gather.3.cloned.1.call-start = ((), (), s32[]{:S(2)}) async-start(), calls=%async_computation.9 | async-start | bytes 10616832 | tf_op jit(solution)/shard_map/all_gather | solution.py:231
  74.9 38.6 %all-to-all-start.1 = ((bf16[20,144,512]{2,1,0:T(8,128)(2,1)}), bf16[20,144,512]{2,1,0:T(8,128)(2,1)}, u32[]{:S(2)}, u32[]{:S(2)}) async-start(bf16[20,144,512]{2,1,0:T(8,128)(2,1)} %gather_fusion.2), calls=%async_computation.1 | async-start | bytes 5898240 | tf_op jit(solution)/shard_map/cond/branch_1_fun/all_to_all | solution.py:219
  116.0 1.0 copy-start.6
  117.1 223.2 %reduce-scatter.4.cloned.1.call-start = ((), (), s32[]{:S(2)}) async-start(), calls=%async_computation.11 | async-start | bytes 4128768
  177.6 1.4 copy-start.2
  248.3 1.6 copy-start.3
  249.9 22.4 %copy-start.4 = (bf16[512,2048]{0,1:T(8,128)(2,1)S(1)}, bf16[512,2048]{0,1:T(8,128)(2,1)}, u32[]{:S(2)}) copy-start(bf16[512,2048]{0,1:T(8,128)(2,1)} %copy.26) | copy-start | bytes 6291460
  290.7 51.6 %copy-start.1 = (bf16[512,2048]{1,0:T(8,128)(2,1)S(1)}, bf16[512,2048]{1,0:T(8,128)(2,1)}, u32[]{:S(2)}) copy-start(bf16[512,2048]{1,0:T(8,128)(2,1)} %param.23) | copy-start | bytes 6291460
Sparse Core Ops, SparseCore 0:
  66.3 91.2 all-gather.4
  159.2 89.1 all-gather.2
  296.9 43.3 reduce-scatter.3

commit v2 on v1

--- a/solution.py
+++ b/solution.py
@@ -261,15 +261,13 @@
         jnp.bfloat16
     )
     heads_out = heads_out.reshape(per_group * query_rows, heads_dev * DV)
-    mixed = lax.psum_scatter(
-        lax.dot_general(
-            w_o, heads_out, (((0,), (1,)), ((), ())), preferred_element_type=jnp.float32
-        ).astype(jnp.bfloat16),
-        "dev",
-        scatter_dimension=0,
-        tiled=True,
-    )
-    return mixed.T
+    w_out = w_o.reshape(w_o.shape[0], columns, w_o.shape[1] // columns)
+    half = heads_out.shape[0] // 2
+    mixed = []
+    for part in (heads_out[:half], heads_out[half:]):
+        share = jnp.einsum("rk,kcd->crd", part, w_out, preferred_element_type=jnp.float32)
+        mixed.append(lax.psum_scatter(share.astype(jnp.bfloat16), "dev", scatter_dimension=0))
+    return jnp.concatenate(mixed, axis=0)
 
 
 def solution(mesh):

time: 346 us -> 368 us (1.064)
  waiting for transfers between devices: 203 us -> 216 us
  matrix products: 22.9 us -> 34.2 us
  local copies, waits for them, and re-layouts: 46.3 us -> 38.5 us
    reduce_scatter x0 -> x2, waiting for transfers between devices: none -> 56.4 us  [local(): lax.psum_scatter(share.astype(jnp.bfloat16), 'dev', scatter_dimension=0)]
    unnamed x4, waiting for transfers between devices: 43.6 us -> 0.07 us
    dot_general x1 -> x2, matrix products: 14.6 us -> 25.9 us  [local(): jnp.einsum('rk,kcd->crd', part, w_out, preferred_element_type=jnp.float32)]
    unnamed x19 -> x17, local copies, waits for them, and re-layouts: 14.3 us -> 6.23 us
  transfers between devices with their start and end apart: 5 -> 6, of which waited for: 5 -> 6; matrix products, arithmetic and copies ran while one was open for 9% -> 12% of each run, Pallas kernels for 6% -> 5%
where the time goes in v2:
time: 368 us; the launch traced here: 367 us
  waiting for transfers between devices  216 us (59%)
  Pallas kernels  42.5 us (12%)
  local copies, waits for them, and re-layouts  38.5 us (10%)
  matrix products  34.2 us (9%)
  between operations  15.3 us (4%)
  starting transfers between devices  10.2 us (3%)
  other arithmetic  10.1 us (3%)
    all_gather x2, waiting for transfers between devices, local(): gathered = [lax.all_gather(o, 'dev', axis=0, tiled=True) for o in own]  90.9 us
    all_to_all x2, waiting for transfers between devices, exchange(): got = lax.all_to_all(out, 'grp', split_axis=0, concat_axis=0, tiled=True)  68.8 us
    reduce_scatter x2, waiting for transfers between devices, local(): lax.psum_scatter(share.astype(jnp.bfloat16), 'dev', scatter_dimension=0)  56.4 us
    pallas_call x2, Pallas kernels, attention(): pl.pallas_call(functools.partial(attend, first, last, chunk * span, block...  42.5 us
    dot_general x2, matrix products, local(): jnp.einsum('rk,kcd->crd', part, w_out, preferred_element_type=jnp.float32)  25.9 us
    all_to_all x2, starting transfers between devices, exchange(): got = lax.all_to_all(out, 'grp', split_axis=0, concat_axis=0, tiled=True)  9.89 us
    gather x2, local copies, waits for them, and re-layouts, exchange(): out = packed[index]  8.29 us
  transfers between devices with their start and end apart: 6, of which 6 were waited for; matrix products, arithmetic and copies ran while one was open for 12% of the time, Pallas kernels for 5%

profile of v2, /device:TPU:0, one launch (start us, length us, event | category | flops | bytes accessed | tf_op | source)
XLA Modules:
  0.0 367.2 jit_solution(11511350513388726955)
XLA Ops:
  6.5 0.9 iota_compare_fusion.10
  7.4 0.9 select_reduce_fusion.10
  8.3 0.1 broadcast_compare_fusion
  8.3 0.1 lt.220
  8.5 0.7 broadcast_in_dim.296
  9.2 0.1 reshape.414
  9.3 1.3 select_reduce_fusion.8
  10.6 0.1 reshape.415
  10.8 0.3 convert_reduce_fusion
  11.0 0.6 select_reduce_fusion.15
  13.6 0.1 select_reduce_fusion.11
  13.8 51.3 %conditional.3 = (bf16[8,144,512]{2,1,0:T(8,128)(2,1)S(1)}) conditional(s32[]{:T(128)} %clamp.4, (bf16[16,256,512]{2,1,0:T(8,128)(2,1)}, bf16[16,64,256]{2,1,0:T(8,128)(2,1)}, s32[256]{0:T(256)S(1)}, pred[256]{0:T(512)(128)(4,1)S(1)}, s32[256]{0:T(256)S(1)}, /*index=5*/s32[256]{0:T(256)S(1)}, s32[8]{0:T(128)S(1)}, ...), branch_computations={%region_19.21_spmd, %region_21.23_spmd, %region_23.25_spmd, %regio... | conditional | flops 11824488 | bytes 35403848 | solution.py:230
  13.8 1.0 fusion.34
  14.8 1.8 slice.69
  16.6 0.1 select_reduce_fusion.5
  16.7 1.6 maximum_maximum_fusion.5
  18.3 4.2 %gather_fusion.10 = bf16[20,144,512]{2,1,0:T(8,128)(2,1)} fusion(bf16[16,144,512]{2,1,0:T(8,128)(2,1)} %maximum_maximum_fusion.5, s32[1024]{0:T(1024)S(1)} %pad_clamp_fusion.11), kind=kCustom, calls=%fused_computation.10 | custom fusion | bytes 5898320 | tf_op jit(solution)/shard_map/cond/branch_1_fun/gather | solution.py:218
  22.4 5.2 %all-to-all-start.5 = ((bf16[20,144,512]{2,1,0:T(8,128)(2,1)}), bf16[20,144,512]{2,1,0:T(8,128)(2,1)}, u32[]{:S(2)}, u32[]{:S(2)}) async-start(bf16[20,144,512]{2,1,0:T(8,128)(2,1)} %gather_fusion.10), calls=%async_computation.5 | async-start | bytes 5898240 | tf_op jit(solution)/shard_map/cond/branch_1_fun/all_to_all | solution.py:219
  27.7 35.0 %all-to-all-done.5 = bf16[20,144,512]{2,1,0:T(8,128)(2,1)} async-done(((bf16[20,144,512]{2,1,0:T(8,128)(2,1)}), bf16[20,144,512]{2,1,0:T(8,128)(2,1)}, u32[]{:S(2)}, u32[]{:S(2)}) %all-to-all-start.5) | async-done | bytes 2949152 | tf_op jit(solution)/shard_map/cond/branch_1_fun/all_to_all | solution.py:219
  62.6 2.5 gather_fusion.11
  65.1 1.0 copy-done.5
  66.1 0.0 all-gather.5.cloned.1.call-update
  66.2 0.0 copy-start.7
  66.2 0.0 all-gather.3.cloned.1.call-start
  66.2 49.8 %conditional.2 = (bf16[8,144,512]{2,1,0:T(8,128)(2,1)S(1)}) conditional(s32[]{:T(128)} %clamp.4, (bf16[16,256,512]{2,1,0:T(8,128)(2,1)}, bf16[16,64,256]{2,1,0:T(8,128)(2,1)}, s32[256]{0:T(256)S(1)}, pred[256]{0:T(512)(128)(4,1)S(1)}, s32[256]{0:T(256)S(1)}, /*index=5*/s32[256]{0:T(256)S(1)}, s32[8]{0:T(128)S(1)}, ...), branch_computations={%region_11.13_spmd, %region_13.15_spmd, %region_15.17_spmd, %regio... | conditional | flops 11824488 | bytes 35403848 | solution.py:230
  66.3 1.0 fusion.30
  67.2 1.8 slice.65
  69.1 0.1 select_reduce_fusion.1
  69.2 1.6 maximum_maximum_fusion.1
  70.8 4.1 %gather_fusion.2 = bf16[20,144,512]{2,1,0:T(8,128)(2,1)} fusion(bf16[16,144,512]{2,1,0:T(8,128)(2,1)} %maximum_maximum_fusion.1, s32[1024]{0:T(1024)S(1)} %pad_clamp_fusion.3), kind=kCustom, calls=%fused_computation.2 | custom fusion | bytes 5898320 | tf_op jit(solution)/shard_map/cond/branch_1_fun/gather | solution.py:218
  74.9 4.7 %all-to-all-start.1 = ((bf16[20,144,512]{2,1,0:T(8,128)(2,1)}), bf16[20,144,512]{2,1,0:T(8,128)(2,1)}, u32[]{:S(2)}, u32[]{:S(2)}) async-start(bf16[20,144,512]{2,1,0:T(8,128)(2,1)} %gather_fusion.2), calls=%async_computation.1 | async-start | bytes 5898240 | tf_op jit(solution)/shard_map/cond/branch_1_fun/all_to_all | solution.py:219
  79.6 33.8 %all-to-all-done.1 = bf16[20,144,512]{2,1,0:T(8,128)(2,1)} async-done(((bf16[20,144,512]{2,1,0:T(8,128)(2,1)}), bf16[20,144,512]{2,1,0:T(8,128)(2,1)}, u32[]{:S(2)}, u32[]{:S(2)}) %all-to-all-start.1) | async-done | bytes 2949152 | tf_op jit(solution)/shard_map/cond/branch_1_fun/all_to_all | solution.py:219
  113.5 2.5 gather_fusion.3
  116.1 1.0 copy-done.6
  117.1 0.0 all-gather.3.cloned.1.call-update
  117.1 0.2 reduce-scatter.3.cloned.1.call-start
  117.3 0.2 convert_reduce_fusion.2
  117.5 0.1 iota_add_fusion
  117.6 0.1 add.259
  117.7 0.1 select_reduce_fusion.13
  117.9 2.9 gather_fusion.16
  120.7 1.2 copy.49
  122.0 2.2 gather_fusion.17
  124.1 1.6 reshape.420
  125.8 1.5 copy.69
  127.3 3.9 %copy.44 = bf16[512,2048]{0,1:T(8,128)(2,1)} copy(bf16[512,2048]{1,0:T(8,128)(2,1)} %param.24) | data formatting | bytes 4194304 | tf_op jit(solution)/shard_map/reshape | solution.py:259
  131.2 0.1 select_reduce_fusion.9.where
  131.3 4.6 %convolution_convert_fusion.refs_0_ = bf16[16,256,512]{2,1,0:T(8,128)(2,1)} fusion(bf16[256,16,128]{2,1,0:T(8,128)(2,1)} %bitcast.84, bf16[512,2048]{1,0:T(8,128)(2,1)S(1)} %copy-done), kind=kOutput, calls=%fused_computation.96 | convolution fusion | flops 538968064 | bytes 7340032 | tf_op jit(solution)/shard_map/qhn,chn->hqc/dot_general | solution.py:238
  136.0 21.6 %all-gather.5.cloned.1.call-done.refs_2_.refs_3_.refs_4_.refs_5_.refs_6_.refs_7_.refs_8_.refs_9_ = bf16[64,144,512]{2,1,0:T(8,128)(2,1)} async-done(((bf16[8,144,512]{2,1,0:T(8,128)(2,1)}), bf16[64,144,512]{2,1,0:T(8,128)(2,1)}) %all-gather.5.cloned.1.call-update) | async-done | bytes 9437200 | tf_op jit(solution)/shard_map/all_gather | solution.py:231
  157.5 20.1 %attend0.1 = (f32[16,256,512]{2,1,0:T(8,128)}, f32[16,256,128]{2,1,0:T(8,128)S(1)}, f32[16,256,128]{2,1,0:T(8,128)S(1)}) custom-call(s32[64]{0:T(128)S(1)} %select_reduce_fusion.9.where, s32[8]{0:T(128)S(1)} %get-tuple-element.218.sizes, bf16[16,256,512]{2,1,0:T(8,128)(2,1)} %convolution_convert_fusion.refs_0_, bf16[16,256,64]{2,1,0:T(8,128)(2,1)S(1)} %bitcast.81, ...), custom_call_target="tpu_custom_call" | custom-call | flops 9126805504 | bytes 26214400 | tf_op jit(solution)/shard_map/attend0/pallas_call | solution.py:107
  177.6 1.3 copy-done.2
  179.0 69.4 %all-gather.3.cloned.1.call-done.refs_2_.refs_3_.refs_4_.refs_5_.refs_6_.refs_7_.refs_8_.refs_9_ = bf16[64,144,512]{2,1,0:T(8,128)(2,1)} async-done(((bf16[8,144,512]{2,1,0:T(8,128)(2,1)}), bf16[64,144,512]{2,1,0:T(8,128)(2,1)}) %all-gather.3.cloned.1.call-update) | async-done | bytes 9437200 | tf_op jit(solution)/shard_map/all_gather | solution.py:231
  248.3 1.6 copy-done.3
  249.9 22.4 %attend1.1 = bf16[16,256,512]{2,1,0:T(8,128)(2,1)} custom-call(s32[64]{0:T(128)S(1)} %select_reduce_fusion.9.where, s32[8]{0:T(128)S(1)} %get-tuple-element.218.sizes, bf16[16,256,512]{2,1,0:T(8,128)(2,1)} %convolution_convert_fusion.refs_0_, bf16[16,256,64]{2,1,0:T(8,128)(2,1)S(1)} %bitcast.82, ...), custom_call_target="tpu_custom_call" | custom-call | flops 9126805504 | bytes 26214400 | tf_op jit(solution)/shard_map/attend1/pallas_call | solution.py:107
  272.4 3.7 fusion.20
  276.0 0.3 fusion.37
  276.3 12.8 %convert_bitcast_fusion.1 = bf16[8,128,896]{2,1,0:T(8,128)(2,1)} fusion(bf16[128,2048,1]{0,1,2:T(8,128)(2,1)S(1)} %bitcast.87, bf16[256,8,8,896]{3,2,1,0:T(8,128)(2,1)} %bitcast.93), kind=kOutput, calls=%fused_computation.100 | convolution fusion | flops 3759013888 | bytes 31719424 | tf_op jit(solution)/shard_map/rk,kcd->crd/dot_general | solution.py:268
  289.1 0.0 reduce-scatter.3.cloned.1.call-update
  289.2 0.0 reduce-scatter.5.cloned.1.call-start
  289.2 13.1 %convert_bitcast_fusion = bf16[8,128,896]{2,1,0:T(8,128)(2,1)} fusion(bf16[128,2048,1]{0,1,2:T(8,128)(2,1)S(1)} %bitcast.86, bf16[256,8,8,896]{3,2,1,0:T(8,128)(2,1)} %bitcast.94), kind=kOutput, calls=%fused_computation.99 | convolution fusion | flops 3759013888 | bytes 31719424 | tf_op jit(solution)/shard_map/rk,kcd->crd/dot_general | solution.py:268
  302.4 0.0 reduce-scatter.5.cloned.1.call-update
  302.4 20.9 %reduce-scatter.3.cloned.1.call-done = bf16[1,128,896]{2,1,0:T(8,128)(2,1)} async-done(((bf16[8,128,896]{2,1,0:T(8,128)(2,1)}), bf16[1,128,896]{2,1,0:T(8,128)(2,1)}) %reduce-scatter.3.cloned.1.call-update) | async-done | bytes 229392 | tf_op jit(solution)/shard_map/reduce_scatter | solution.py:269
  323.3 35.5 %reduce-scatter.5.cloned.1.call-done = bf16[1,128,896]{2,1,0:T(8,128)(2,1)} async-done(((bf16[8,128,896]{2,1,0:T(8,128)(2,1)}), bf16[1,128,896]{2,1,0:T(8,128)(2,1)}) %reduce-scatter.5.cloned.1.call-update) | async-done | bytes 229392 | tf_op jit(solution)/shard_map/reduce_scatter | solution.py:269
  358.8 1.9 pad_maximum_fusion
  (32 shorter events, 0.2 us)
Async XLA Ops:
  6.5 124.8 %copy-start = (bf16[512,2048]{1,0:T(8,128)(2,1)S(1)}, bf16[512,2048]{1,0:T(8,128)(2,1)}, u32[]{:S(2)}) copy-start(bf16[512,2048]{1,0:T(8,128)(2,1)} %param.23) | copy-start | bytes 6291460
  6.5 151.0 %all-gather.5.cloned.1.call-start = ((), (), s32[]{:S(2)}) async-start(), calls=%async_computation.11 | async-start | bytes 10616832 | tf_op jit(solution)/shard_map/all_gather | solution.py:231
  22.4 40.2 %all-to-all-start.5 = ((bf16[20,144,512]{2,1,0:T(8,128)(2,1)}), bf16[20,144,512]{2,1,0:T(8,128)(2,1)}, u32[]{:S(2)}, u32[]{:S(2)}) async-start(bf16[20,144,512]{2,1,0:T(8,128)(2,1)} %gather_fusion.10), calls=%async_computation.5 | async-start | bytes 5898240 | tf_op jit(solution)/shard_map/cond/branch_1_fun/all_to_all | solution.py:219
  65.1 1.0 copy-start.5
  66.2 51.1 %copy-start.7 = (s32[32]{0:T(128)S(1)}, s32[32]{0:T(128)}, u32[]{:S(2)}) copy-start(s32[32]{0:T(128)} %param.29) | copy-start | bytes 388
  66.2 182.2 %all-gather.3.cloned.1.call-start = ((), (), s32[]{:S(2)}) async-start(), calls=%async_computation.10 | async-start | bytes 10616832 | tf_op jit(solution)/shard_map/all_gather | solution.py:231
  74.9 38.6 %all-to-all-start.1 = ((bf16[20,144,512]{2,1,0:T(8,128)(2,1)}), bf16[20,144,512]{2,1,0:T(8,128)(2,1)}, u32[]{:S(2)}, u32[]{:S(2)}) async-start(bf16[20,144,512]{2,1,0:T(8,128)(2,1)} %gather_fusion.2), calls=%async_computation.1 | async-start | bytes 5898240 | tf_op jit(solution)/shard_map/cond/branch_1_fun/all_to_all | solution.py:219
  116.0 1.0 copy-start.6
  117.1 206.2 %reduce-scatter.3.cloned.1.call-start = ((), (), s32[]{:S(2)}) async-start(), calls=%async_computation.12 | async-start | bytes 2064384 | tf_op jit(solution)/shard_map/reduce_scatter | solution.py:269
  177.6 1.4 copy-start.2
  248.3 1.6 copy-start.3
  249.9 22.4 %copy-start.4 = (bf16[512,2048]{0,1:T(8,128)(2,1)S(1)}, bf16[512,2048]{0,1:T(8,128)(2,1)}, u32[]{:S(2)}) copy-start(bf16[512,2048]{0,1:T(8,128)(2,1)} %copy.44) | copy-start | bytes 6291460
  289.2 69.7 %reduce-scatter.5.cloned.1.call-start = ((), (), s32[]{:S(2)}) async-start(), calls=%async_computation.13 | async-start | bytes 2064384 | tf_op jit(solution)/shard_map/reduce_scatter | solution.py:269
  289.2 71.5 %copy-start.1 = (bf16[512,2048]{1,0:T(8,128)(2,1)S(1)}, bf16[512,2048]{1,0:T(8,128)(2,1)}, u32[]{:S(2)}) copy-start(bf16[512,2048]{1,0:T(8,128)(2,1)} %param.23) | copy-start | bytes 6291460
Sparse Core Ops, SparseCore 0:
  66.3 91.2 all-gather.4
  159.2 89.1 all-gather.2
  289.3 33.9 reduce-scatter.2
  325.5 33.3 reduce-scatter.4
